TPU v7x, 128 devices: a whole 4x4x4 slice. The times are simulated.
128 devices in a mesh: section: 4 (over y_hi, core), seq: 32 (over y_lo, x, z).
Axes of the slice: x: 4, y: 4 (y_hi: 2, y_lo: 2; y = y_hi * 2 + y_lo), z: 4, core: 2. Of those that a mesh axis runs over, the one named last changes fastest.
Arguments:
- activations: bfloat16 [4, 4352, 1024], P('section', 'seq'), may hold values from -60 to 60
- incoming: bfloat16 [4, 4352, 1024], P('section', 'seq'), may hold values from -6 to 6
- w_query: bfloat16 [4, 1024, 512], P('section'), may hold values from -0.1875 to 0.1875
- w_key: bfloat16 [4, 1024, 512], P('section'), may hold values from -0.1875 to 0.1875
- w_value: bfloat16 [4, 1024, 512], P('section'), may hold values from -0.1875 to 0.1875
- w_out: bfloat16 [4, 512, 2048], P('section'), may hold values from -0.25 to 0.25
- block_ids: int32 [4352], replicated, may hold values from 0 to 135, never falling along the last dimension, each value on 1 to 256 neighbouring positions
- flip_order: int32 [4, 136], P('section'), may hold values from 0 to 135, each once within a row
Outputs:
- carry_out: bfloat16 [4, 4352, 1024], P('section', 'seq')
- grad_query: float32 [4, 1024, 512], P('section', 'seq')
- grad_key: float32 [4, 1024, 512], P('section', 'seq')
- grad_value: float32 [4, 1024, 512], P('section', 'seq')
- grad_out: float32 [4, 512, 2048], P('section', 'seq')
Inputs may be any that keep to these rules, and one draw needn't show every extreme that they name: `block_ids`: block ids never fall along the sequence; each block holds 1 to 256 tokens, one exactly 256. `flip_order`: each row is a permutation.
All inputs are finite; a program needn't handle non-finite values.
Results may differ from a plain program's by a relative error of at most 0.03.
Values may be sent and summed in bfloat16 or wider, within the bound.
A program may use at most 128 MiB of HBM per device.

v0:
```python
import jax
import jax.numpy as jnp
from jax import lax
from jax.sharding import PartitionSpec as P

HEADS = 8
HEAD_DIM = 64
EPSILON = 1e-06


def partner(block, axis, stride):
    count = lax.axis_size(axis)
    route = []
    for low in range(count):
        high = low | 1 << stride
        if high != low and high < count:
            route += [(low, high), (high, low)]
    return lax.ppermute(block, axis, route)


def shifted(block, axis, distance):
    devices = range(lax.axis_size(axis))
    route = [(i - distance, i) for i in devices if i - distance in devices]
    return lax.ppermute(block, axis, route)


def split_heads(matrix):
    return matrix.reshape(matrix.shape[0], HEADS, HEAD_DIM)


def head_major(matrix):
    return jnp.transpose(split_heads(matrix), (1, 0, 2))


def unit_heads(projected):
    parts = split_heads(projected)
    factor = lax.rsqrt(jnp.mean(parts * parts, axis=-1, keepdims=True) + EPSILON)
    return (parts * factor, factor)


def unit_back(grad_heads, unit, factor):
    return factor * (grad_heads - unit * jnp.mean(grad_heads * unit, axis=-1, keepdims=True))


def mirror(rows):
    for bit in range(lax.axis_size("seq").bit_length() - 1):
        rows = partner(rows, "seq", bit)
    return rows


def to_previous(rows):
    return shifted(rows, "section", -1)


def shards(activations, incoming, w_query, w_key, w_value, w_out, block_ids, flip_order):
    field = activations[0].astype(jnp.float32)
    upstream = incoming[0].astype(jnp.float32)
    weight_query = w_query[0]
    weight_key = w_key[0]
    weight_value = w_value[0]
    weight_out = w_out[0]
    flip_row = flip_order[0]
    rows = field.shape[0]
    width = field.shape[1]
    inner = weight_query.shape[1]
    scale = HEAD_DIM ** (-0.5)
    first = lax.axis_index("seq") * rows
    my_blocks = lax.dynamic_slice_in_dim(block_ids, first, rows)
    row_scale = lax.rsqrt(jnp.mean(field * field, axis=-1, keepdims=True) + EPSILON)
    unit_rows = field * row_scale
    normed = unit_rows.astype(jnp.bfloat16)
    query_raw = jnp.dot(normed, weight_query, preferred_element_type=jnp.float32)
    key_raw = jnp.dot(normed, weight_key, preferred_element_type=jnp.float32)
    values = jnp.dot(normed, weight_value, preferred_element_type=jnp.float32).astype(jnp.bfloat16)
    query_unit, query_scale = unit_heads(query_raw)
    key_unit, key_scale = unit_heads(key_raw)
    queries = query_unit.astype(jnp.bfloat16).reshape(rows, inner)
    keys = key_unit.astype(jnp.bfloat16).reshape(rows, inner)
    keys_all, values_all = (
        lax.all_gather(keys, "seq", axis=0, tiled=True),
        lax.all_gather(values, "seq", axis=0, tiled=True),
    )
    allowed = block_ids[None, :] <= my_blocks[:, None]
    query_heads = head_major(queries)
    key_heads_all = head_major(keys_all)
    value_heads_all = head_major(values_all)

    def probabilities(query_part, key_part):
        scores = jnp.dot(query_part, key_part.T, preferred_element_type=jnp.float32) * scale
        numerator = jnp.where(allowed, jnp.exp(scores), 0.0)
        denominator = jnp.sum(numerator, axis=-1, keepdims=True)
        return (numerator / denominator, denominator)

    def forward_head(operands):
        query_part, key_part, value_part = operands
        probs, denominator = probabilities(query_part, key_part)
        out_part = jnp.dot(
            probs.astype(jnp.bfloat16), value_part, preferred_element_type=jnp.float32
        ).astype(jnp.bfloat16)
        return (out_part, denominator[:, 0])

    heads_out, denominators = lax.map(forward_head, (query_heads, key_heads_all, value_heads_all))
    attended = jnp.transpose(heads_out, (1, 0, 2)).reshape(rows, inner)
    affine = jnp.dot(attended, weight_out, preferred_element_type=jnp.float32)
    shift_part = affine[:, :width]
    log_scale = affine[:, width:]
    factor = jnp.exp(-log_scale)
    latent = (field - shift_part) * factor
    grad_affine = jnp.concatenate([-upstream * factor, 1.0 - upstream * latent], axis=-1).astype(
        jnp.bfloat16
    )
    out_term = jnp.dot(attended.T, grad_affine, preferred_element_type=jnp.float32)
    grad_attn = jnp.dot(grad_affine, weight_out.T, preferred_element_type=jnp.float32).astype(
        jnp.bfloat16
    )
    correction = jnp.sum(
        split_heads(grad_attn.astype(jnp.float32)) * split_heads(attended.astype(jnp.float32)),
        axis=-1,
    )
    grad_heads = head_major(grad_attn)
    correction_heads = jnp.transpose(correction)[:, :, None]

    def backward_head(operands):
        query_part, key_part, value_part, grad_part, corr_part = operands
        probs, denominator = probabilities(query_part, key_part)
        grad_probs = jnp.dot(grad_part, value_part.T, preferred_element_type=jnp.float32)
        grad_scores = (probs * (grad_probs - corr_part)).astype(jnp.bfloat16)
        grad_qpart = jnp.dot(grad_scores, key_part, preferred_element_type=jnp.float32) * scale
        grad_kpart = jnp.dot(grad_scores.T, query_part, preferred_element_type=jnp.float32) * scale
        grad_vpart = jnp.dot(
            probs.astype(jnp.bfloat16).T, grad_part, preferred_element_type=jnp.float32
        )
        return (grad_qpart, grad_kpart, grad_vpart)

    grad_qheads, grad_kall, grad_vall = lax.map(
        backward_head, (query_heads, key_heads_all, value_heads_all, grad_heads, correction_heads)
    )
    key_terms = jnp.transpose(grad_kall, (1, 0, 2)).reshape(-1, inner)
    value_terms = jnp.transpose(grad_vall, (1, 0, 2)).reshape(-1, inner)
    grad_kunit, grad_vsum = (
        lax.psum_scatter(
            key_terms.astype(jnp.bfloat16), "seq", scatter_dimension=0, tiled=True
        ).astype(jnp.float32),
        lax.psum_scatter(
            value_terms.astype(jnp.bfloat16), "seq", scatter_dimension=0, tiled=True
        ).astype(jnp.float32),
    )
    grad_queries = (
        unit_back(jnp.transpose(grad_qheads, (1, 0, 2)), query_unit, query_scale)
        .reshape(rows, inner)
        .astype(jnp.bfloat16)
    )
    grad_keys = (
        unit_back(split_heads(grad_kunit), key_unit, key_scale)
        .reshape(rows, inner)
        .astype(jnp.bfloat16)
    )
    grad_values = grad_vsum.astype(jnp.bfloat16)
    query_term = jnp.dot(normed.T, grad_queries, preferred_element_type=jnp.float32)
    key_term = jnp.dot(normed.T, grad_keys, preferred_element_type=jnp.float32)
    value_term = jnp.dot(normed.T, grad_values, preferred_element_type=jnp.float32)
    sums = (
        lax.psum_scatter(
            query_term.astype(jnp.bfloat16), "seq", scatter_dimension=0, tiled=True
        ).astype(jnp.float32),
        lax.psum_scatter(
            key_term.astype(jnp.bfloat16), "seq", scatter_dimension=0, tiled=True
        ).astype(jnp.float32),
        lax.psum_scatter(
            value_term.astype(jnp.bfloat16), "seq", scatter_dimension=0, tiled=True
        ).astype(jnp.float32),
        lax.psum_scatter(
            out_term.astype(jnp.bfloat16), "seq", scatter_dimension=0, tiled=True
        ).astype(jnp.float32),
    )
    grad_normed = jnp.dot(grad_queries, weight_query.T, preferred_element_type=jnp.float32)
    grad_normed = grad_normed + jnp.dot(grad_keys, weight_key.T, preferred_element_type=jnp.float32)
    grad_normed = grad_normed + jnp.dot(
        grad_values, weight_value.T, preferred_element_type=jnp.float32
    )
    grad_input = upstream * factor + row_scale * (
        grad_normed - unit_rows * jnp.mean(grad_normed * unit_rows, axis=-1, keepdims=True)
    )
    grad_input = grad_input.astype(jnp.bfloat16)
    moved = mirror(to_previous(grad_input))
    carry = jnp.take(moved, flip_row, axis=0)
    return (carry[None], sums[0][None], sums[1][None], sums[2][None], sums[3][None])


def solution(mesh):
    in_specs = (
        P("section", "seq", None),
        P("section", "seq", None),
        P("section", None, None),
        P("section", None, None),
        P("section", None, None),
        P("section", None, None),
        P(),
        P("section", None),
    )
    out_specs = (
        P("section", "seq", None),
        P("section", "seq", None),
        P("section", "seq", None),
        P("section", "seq", None),
        P("section", "seq", None),
    )
    return jax.shard_map(shards, mesh=mesh, in_specs=in_specs, out_specs=out_specs, check_vma=False)
```

profile of v0, /device:TPU:0, one launch (start us, length us, event | category | flops | bytes accessed | tf_op | source)
XLA Modules:
  0.0 1467.9 jit_solution(6070266999776228398)
XLA Ops:
  8.5 2.3 copy.43
  16.0 2.3 convolution_convert_fusion.4
  22.7 153.8 %all-gather.3.cloned.1.call-done = bf16[4352,512]{1,0:T(8,128)(2,1)} async-done(((bf16[136,512]{1,0:T(8,128)(2,1)}), bf16[4352,512]{1,0:T(8,128)(2,1)}) %all-gather.3.cloned.1.call-update) | async-done | bytes 4456464 | tf_op jit(solution)/shard_map/all_gather | solution.py:80
  176.5 6.5 copy.45
  183.0 9.2 copy.48
  192.2 144.8 %all-gather.5.cloned.1.call-done = bf16[4352,512]{1,0:T(8,128)(2,1)} async-done(((bf16[136,512]{1,0:T(8,128)(2,1)}), bf16[4352,512]{1,0:T(8,128)(2,1)}) %all-gather.5.cloned.1.call-update) | async-done | bytes 4456464 | tf_op jit(solution)/shard_map/all_gather | solution.py:81
  337.1 6.5 copy.46
  343.5 9.2 copy.49
  352.7 31.7 %while.26 = (s32[]{:T(128)}, bf16[8,136,64]{1,2,0:T(8,128)(2,1)S(1)}, bf16[8,136,64]{2,1,0:T(8,128)(2,1)S(1)}, bf16[8,4352,64]{2,1,0:T(8,128)(2,1)}, bf16[8,4352...) while((s32[]{:T(128)}, bf16[8,136,64]{1,2,0:T(8,128)(2,1)S(1)}, ...), condition=%wide.region_5.6_spmd.clone, body=%wide.region_3.5_spmd.clone.sunk | while | flops 155079040 | bytes 7055989 | solution.py:102
  394.2 76.1 %while.27 = (s32[]{:T(128)}, f32[8,136,64]{1,2,0:T(8,128)}, bf16[8,4352,64]{1,2,0:T(8,128)(2,1)}, bf16[8,4352,64]{1,2,0:T(8,128)(2,1)}, bf16[8,136,64]{2,1,0:T(8...) while((s32[]{:T(128)}, f32[8,136,64]{1,2,0:T(8,128)}, ...), condition=%wide.region_9.10_spmd.clone, body=%wide.region_7.9_spmd.clone.sunk | while | flops 385003904 | bytes 16456953 | solution.py:135
  394.2 2.0 fusion.147
  401.3 2.5 fusion.149
  410.8 2.5 fusion.149
  420.2 2.5 fusion.149
  429.7 2.5 fusion.149
  439.3 2.5 fusion.149
  448.8 2.5 fusion.149
  458.3 2.5 fusion.149
  467.8 2.5 fusion.149
  470.3 6.6 copy.56
  476.9 6.5 copy.58
  486.5 2.1 convolution_convert_fusion
  488.8 158.3 %reduce-scatter.19.cloned.1.call-done = bf16[136,512]{1,0:T(8,128)(2,1)} async-done(((bf16[4352,512]{1,0:T(8,128)(2,1)}), bf16[136,512]{1,0:T(8,128)(2,1)}) %reduce-scatter.19.cloned.1.call-update) | async-done | bytes 139280
  653.4 161.8 %reduce-scatter.21.cloned.1.call-done = bf16[136,512]{1,0:T(8,128)(2,1)} async-done(((bf16[4352,512]{1,0:T(8,128)(2,1)}), bf16[136,512]{1,0:T(8,128)(2,1)}) %reduce-scatter.21.cloned.1.call-update) | async-done | bytes 139280
  818.7 2.2 collective-permute-done
  822.5 5.4 collective-permute-done.1
  827.9 8.1 collective-permute-done.2
  836.1 6.9 collective-permute-done.3
  843.0 133.7 %reduce-scatter.11.cloned.1.call-done = bf16[32,512]{1,0:T(8,128)(2,1)} async-done(((bf16[1024,512]{1,0:T(8,128)(2,1)}), bf16[32,512]{1,0:T(8,128)(2,1)}) %reduce-scatter.11.cloned.1.call-update) | async-done | bytes 32784 | tf_op jit(solution)/shard_map/reduce_scatter | solution.py:163
  978.2 161.6 %reduce-scatter.17.cloned.1.call-done = bf16[16,2048]{1,0:T(8,128)(2,1)} async-done(((bf16[512,2048]{1,0:T(8,128)(2,1)}), bf16[16,2048]{1,0:T(8,128)(2,1)}) %reduce-scatter.17.cloned.1.call-update) | async-done | bytes 65552 | tf_op jit(solution)/shard_map/reduce_scatter | solution.py:172
  1143.0 157.0 %reduce-scatter.13.cloned.1.call-done = bf16[32,512]{1,0:T(8,128)(2,1)} async-done(((bf16[1024,512]{1,0:T(8,128)(2,1)}), bf16[32,512]{1,0:T(8,128)(2,1)}) %reduce-scatter.13.cloned.1.call-update) | async-done | bytes 32784 | tf_op jit(solution)/shard_map/reduce_scatter | solution.py:166
  1301.4 158.3 %reduce-scatter.15.cloned.1.call-done = bf16[32,512]{1,0:T(8,128)(2,1)} async-done(((bf16[1024,512]{1,0:T(8,128)(2,1)}), bf16[32,512]{1,0:T(8,128)(2,1)}) %reduce-scatter.15.cloned.1.call-update) | async-done | bytes 32784 | tf_op jit(solution)/shard_map/reduce_scatter | solution.py:169
  (176 shorter events, 128.3 us)
Async XLA Ops:
  7.2 379.8 %copy-start = (bf16[1,512,2048]{2,1,0:T(8,128)(2,1)S(1)}, bf16[1,512,2048]{2,1,0:T(8,128)(2,1)}, u32[]{:S(2)}) copy-start(bf16[1,512,2048]{2,1,0:T(8,128)(2,1)} %param.17) | copy-start | bytes 6291460
  7.2 3.6 copy-start.2
  7.2 169.3 %all-gather.3.cloned.1.call-start = ((), (), s32[]{:S(2)}) async-start(), calls=%async_computation.6 | async-start | bytes 4595712 | tf_op jit(solution)/shard_map/all_gather | solution.py:80
  10.8 7.6 copy-start.7
  16.0 321.1 %all-gather.5.cloned.1.call-start = ((), (), s32[]{:S(2)}) async-start(), calls=%async_computation.7 | async-start | bytes 4595712 | tf_op jit(solution)/shard_map/all_gather | solution.py:81
  18.3 628.8 %reduce-scatter.19.cloned.1.call-start = ((), (), s32[]{:S(2)}) async-start(), calls=%async_computation.12 | async-start | bytes 4595712
  18.4 4.2 copy-start.23
  21.5 0.8 copy-start.5
  343.5 9.2 copy-start.21
  476.9 338.3 %reduce-scatter.21.cloned.1.call-start = ((), (), s32[]{:S(2)}) async-start(), calls=%async_computation.13 | async-start | bytes 4595712
  483.4 1.0 copy-start.6
  483.4 1.2 copy-start.12
  483.4 493.3 %reduce-scatter.11.cloned.1.call-start = ((), (), s32[]{:S(2)}) async-start(), calls=%async_computation.8 | async-start | bytes 1081344 | tf_op jit(solution)/shard_map/reduce_scatter | solution.py:163
  484.6 1.8 copy-start.13
  484.6 1.8 copy-start.16
  484.6 1.9 copy-start.18
  486.4 161.8 %copy-start.4 = (f32[136,8,64]{0,2,1:T(8,128)S(1)}, f32[136,8,64]{0,2,1:T(8,128)}, u32[]{:S(2)}) copy-start(f32[136,8,64]{0,2,1:T(8,128)} %copy-done.3) | copy-start | bytes 835588
  486.4 653.4 %reduce-scatter.17.cloned.1.call-start = ((), (), s32[]{:S(2)}) async-start(), calls=%async_computation.11 | async-start | bytes 2162688 | tf_op jit(solution)/shard_map/reduce_scatter | solution.py:172
  488.6 162.2 %copy-start.8 = (bf16[1,1024,512]{2,1,0:T(8,128)(2,1)S(1)}, bf16[1,1024,512]{2,1,0:T(8,128)(2,1)}, u32[]{:S(2)}) copy-start(bf16[1,1024,512]{2,1,0:T(8,128)(2,1)} %param.14) | copy-start | bytes 3145732
  488.6 811.4 %reduce-scatter.13.cloned.1.call-start = ((), (), s32[]{:S(2)}) async-start(), calls=%async_computation.9 | async-start | bytes 1081344 | tf_op jit(solution)/shard_map/reduce_scatter | solution.py:166
  650.7 0.9 copy-start.11
  650.7 809.0 %reduce-scatter.15.cloned.1.call-start = ((), (), s32[]{:S(2)}) async-start(), calls=%async_computation.10 | async-start | bytes 1081344 | tf_op jit(solution)/shard_map/reduce_scatter | solution.py:169
  651.6 165.5 %copy-start.14 = (bf16[1,136,1024]{2,1,0:T(8,128)(2,1)S(1)}, bf16[1,136,1024]{2,1,0:T(8,128)(2,1)}, u32[]{:S(2)}) copy-start(bf16[1,136,1024]{2,1,0:T(8,128)(2,1)} %param.13) | copy-start | bytes 835588
  815.2 5.7 copy-start.20
  817.1 18.9 %copy-start.22 = (s32[1,136]{1,0:T(1,128)S(1)}, s32[1,136]{1,0:T(1,128)}, u32[]{:S(2)}) copy-start(s32[1,136]{1,0:T(1,128)} %param.19) | copy-start | bytes 1636
  817.4 3.5 collective-permute-start
  820.9 7.0 collective-permute-start.1
  820.9 640.2 %copy-start.1 = (bf16[1,512,2048]{2,1,0:T(8,128)(2,1)S(1)}, bf16[1,512,2048]{2,1,0:T(8,128)(2,1)}, u32[]{:S(2)}) copy-start(bf16[1,512,2048]{2,1,0:T(8,128)(2,1)} %param.17) | copy-start | bytes 6291460
  827.9 8.1 collective-permute-start.2
  836.1 6.9 collective-permute-start.3
  843.0 135.1 %collective-permute-start.4 = (bf16[136,1024]{1,0:T(8,128)(2,1)S(1)}, bf16[136,1024]{1,0:T(8,128)(2,1)S(1)}, u32[]{:S(2)}, u32[]{:S(2)}) collective-permute-start(bf16[136,1024]{1,0:T(8,128)(2,1)S(1)} %collective-permute-done.3), channel_id=1, source_target_pairs={{0,8},{8,0},{1,9},{9,1},{2,10},{10,2},{3,11},{11,3},{4,12},{12,4},... | collective-permute-start | bytes 835592 | tf_op jit(solution)/shard_map/ppermute | solution.py:18
  978.2 163.2 %collective-permute-start.5 = (bf16[136,1024]{1,0:T(8,128)(2,1)S(1)}, bf16[136,1024]{1,0:T(8,128)(2,1)S(1)}, u32[]{:S(2)}, u32[]{:S(2)}) collective-permute-start(bf16[136,1024]{1,0:T(8,128)(2,1)S(1)} %collective-permute-done.4), channel_id=1, source_target_pairs={{0,16},{16,0},{1,17},{17,1},{2,18},{18,2},{3,19},{19,3},{4,20},{20... | collective-permute-start | bytes 835592 | tf_op jit(solution)/shard_map/ppermute | solution.py:18
  (6 other events, 4.5 us)
Sparse Core Ops, SparseCore 0:
  16.1 160.3 all-gather.2
  178.2 158.8 all-gather.4
  477.0 170.0 reduce-scatter.18
  649.5 165.6 reduce-scatter.20
  817.4 159.3 reduce-scatter.10
  979.1 160.6 reduce-scatter.16
  1142.2 157.7 reduce-scatter.12
  1302.4 157.1 reduce-scatter.14
where the time goes:
time: 1470 us
  waiting for transfers between devices  1250 us (85%)
  matrix products  127 us (9%)
  local copies, waits for them, and re-layouts  60.4 us (4%)
    unnamed x10, waiting for transfers between devices  320 us
    reduce_scatter x1, waiting for transfers between devices, shards(): lax.psum_scatter(out_term.astype(jnp.bfloat16), 'seq', scatter_dimension=...  162 us
    reduce_scatter x1, waiting for transfers between devices, shards(): lax.psum_scatter(value_term.astype(jnp.bfloat16), 'seq', scatter_dimensio...  158 us
    reduce_scatter x1, waiting for transfers between devices, shards(): lax.psum_scatter(key_term.astype(jnp.bfloat16), 'seq', scatter_dimension=...  157 us
    all_gather x1, waiting for transfers between devices, shards(): lax.all_gather(keys, 'seq', axis=0, tiled=True)  154 us
    all_gather x1, waiting for transfers between devices, shards(): lax.all_gather(values, 'seq', axis=0, tiled=True)  145 us
    reduce_scatter x1, waiting for transfers between devices, shards(): lax.psum_scatter(query_term.astype(jnp.bfloat16), 'seq', scatter_dimensio...  134 us
    unnamed x58, local copies, waits for them, and re-layouts  42.5 us
  transfers between devices with their start and end apart: 14, of which 12 were waited for; matrix products, arithmetic and copies ran while one was open for 3% of the time, Pallas kernels for 0%

commit v1 on v0

--- a/solution.py
+++ b/solution.py
@@ -6,6 +6,11 @@
 HEADS = 8
 HEAD_DIM = 64
 EPSILON = 1e-06
+
+
+def gather_over(shard, name, along):
+    sent = jnp.stack([shard] * lax.axis_size(name))
+    return jnp.concatenate(lax.all_to_all(sent, name, 0, 0), axis=along)
 
 
 def partner(block, axis, stride):
@@ -78,7 +83,7 @@
     keys = key_unit.astype(jnp.bfloat16).reshape(rows, inner)
     keys_all, values_all = (
         lax.all_gather(keys, "seq", axis=0, tiled=True),
-        lax.all_gather(values, "seq", axis=0, tiled=True),
+        gather_over(values, "seq", 0),
     )
     allowed = block_ids[None, :] <= my_blocks[:, None]
     query_heads = head_major(queries)

time: 1470 us -> 1360 us (0.925)
  waiting for transfers between devices: 1250 us -> 1120 us
    all_gather x1 -> x0, waiting for transfers between devices: 145 us -> none  [shards(): lax.all_gather(values, 'seq', axis=0, tiled=True)]
    all_to_all x0 -> x1, waiting for transfers between devices: none -> 61.4 us  [gather_over(): return jnp.concatenate(lax.all_to_all(sent, name, 0, 0), axis=along)]
    all_gather x1, waiting for transfers between devices: 154 us -> 110 us  [shards(): lax.all_gather(keys, 'seq', axis=0, tiled=True)]
    unnamed x58 -> x60, local copies, waits for them, and re-layouts: 42.5 us -> 41.4 us
    unnamed x10 -> x9, waiting for transfers between devices: 320 us -> 320 us
  transfers between devices with their start and end apart: 14 -> 14, of which waited for: 12 -> 12; matrix products, arithmetic and copies ran while one was open for 3% -> 4% of each run, Pallas kernels for 0% -> 0%
where the time goes in v1:
time: 1360 us; the launch traced here: 1350 us
  waiting for transfers between devices  1120 us (82%)
  matrix products  125 us (9%)
  local copies, waits for them, and re-layouts  67.1 us (5%)
  between operations  14.5 us (1%)
    unnamed x9, waiting for transfers between devices  320 us
    reduce_scatter x1, waiting for transfers between devices, shards(): lax.psum_scatter(out_term.astype(jnp.bfloat16), 'seq', scatter_dimension=...  161 us
    reduce_scatter x1, waiting for transfers between devices, shards(): lax.psum_scatter(value_term.astype(jnp.bfloat16), 'seq', scatter_dimensio...  159 us
    reduce_scatter x1, waiting for transfers between devices, shards(): lax.psum_scatter(key_term.astype(jnp.bfloat16), 'seq', scatter_dimension=...  156 us
    reduce_scatter x1, waiting for transfers between devices, shards(): lax.psum_scatter(query_term.astype(jnp.bfloat16), 'seq', scatter_dimensio...  134 us
    all_gather x1, waiting for transfers between devices, shards(): lax.all_gather(keys, 'seq', axis=0, tiled=True)  110 us
    all_to_all x1, waiting for transfers between devices, gather_over(): return jnp.concatenate(lax.all_to_all(sent, name, 0, 0), axis=along)  61.4 us
    unnamed x60, local copies, waits for them, and re-layouts  41.4 us
  transfers between devices with their start and end apart: 14, of which 12 were waited for; matrix products, arithmetic and copies ran while one was open for 4% of the time, Pallas kernels for 0%

profile of v1, /device:TPU:0, one launch (start us, length us, event | category | flops | bytes accessed | tf_op | source)
XLA Modules:
  0.0 1353.5 jit_solution(13304122024185574035)
XLA Ops:
  8.5 2.4 copy.42
  16.4 2.3 stack.2
  18.7 9.5 all-to-all-start
  32.6 61.4 %all-to-all-done = bf16[32,136,512]{2,1,0:T(8,128)(2,1)} async-done(((bf16[32,136,512]{2,1,0:T(8,128)(2,1)}), bf16[32,136,512]{2,1,0:T(8,128)(2,1)}, u32[]{:S(2)}, u32[]{:S(2)}) %all-to-all-start) | async-done | bytes 4456480 | tf_op jit(solution)/shard_map/all_to_all | solution.py:13
  94.1 12.1 reshape.215
  106.1 8.1 copy.48
  114.3 109.7 %all-gather.2.cloned.1.call-done = bf16[4352,512]{1,0:T(8,128)(2,1)} async-done(((bf16[136,512]{1,0:T(8,128)(2,1)}), bf16[4352,512]{1,0:T(8,128)(2,1)}) %all-gather.2.cloned.1.call-update) | async-done | bytes 4456464 | tf_op jit(solution)/shard_map/all_gather | solution.py:85
  224.0 6.5 copy.44
  230.4 9.2 copy.47
  239.6 31.7 %while.26 = (s32[]{:T(128)}, bf16[8,136,64]{1,2,0:T(8,128)(2,1)S(1)}, bf16[8,136,64]{2,1,0:T(8,128)(2,1)S(1)}, bf16[8,4352,64]{2,1,0:T(8,128)(2,1)}, bf16[8,4352...) while((s32[]{:T(128)}, bf16[8,136,64]{1,2,0:T(8,128)(2,1)S(1)}, ...), condition=%wide.region_5.6_spmd.clone, body=%wide.region_3.5_spmd.clone.sunk | while | flops 155079040 | bytes 7055989 | solution.py:107
  281.1 76.1 %while.27 = (s32[]{:T(128)}, f32[8,136,64]{1,2,0:T(8,128)}, bf16[8,4352,64]{1,2,0:T(8,128)(2,1)}, bf16[8,4352,64]{1,2,0:T(8,128)(2,1)}, bf16[8,136,64]{2,1,0:T(8...) while((s32[]{:T(128)}, f32[8,136,64]{1,2,0:T(8,128)}, ...), condition=%wide.region_9.10_spmd.clone, body=%wide.region_7.9_spmd.clone.sunk | while | flops 385003904 | bytes 16456953 | solution.py:140
  288.2 2.5 fusion.149
  297.7 2.5 fusion.149
  307.2 2.5 fusion.149
  316.7 2.5 fusion.149
  326.2 2.5 fusion.149
  335.7 2.5 fusion.149
  345.2 2.5 fusion.149
  354.7 2.5 fusion.149
  357.2 6.6 copy.58
  363.8 6.5 copy.60
  373.4 2.1 convolution_convert_fusion
  375.6 157.8 %reduce-scatter.19.cloned.1.call-done = bf16[136,512]{1,0:T(8,128)(2,1)} async-done(((bf16[4352,512]{1,0:T(8,128)(2,1)}), bf16[136,512]{1,0:T(8,128)(2,1)}) %reduce-scatter.19.cloned.1.call-update) | async-done | bytes 139280
  539.6 162.5 %reduce-scatter.21.cloned.1.call-done = bf16[136,512]{1,0:T(8,128)(2,1)} async-done(((bf16[4352,512]{1,0:T(8,128)(2,1)}), bf16[136,512]{1,0:T(8,128)(2,1)}) %reduce-scatter.21.cloned.1.call-update) | async-done | bytes 139280
  705.6 2.2 collective-permute-done
  709.4 5.1 collective-permute-done.1
  714.5 8.1 collective-permute-done.2
  722.7 7.0 collective-permute-done.3
  729.7 134.2 %reduce-scatter.11.cloned.1.call-done = bf16[32,512]{1,0:T(8,128)(2,1)} async-done(((bf16[1024,512]{1,0:T(8,128)(2,1)}), bf16[32,512]{1,0:T(8,128)(2,1)}) %reduce-scatter.11.cloned.1.call-update) | async-done | bytes 32784 | tf_op jit(solution)/shard_map/reduce_scatter | solution.py:168
  865.3 160.6 %reduce-scatter.17.cloned.1.call-done = bf16[16,2048]{1,0:T(8,128)(2,1)} async-done(((bf16[512,2048]{1,0:T(8,128)(2,1)}), bf16[16,2048]{1,0:T(8,128)(2,1)}) %reduce-scatter.17.cloned.1.call-update) | async-done | bytes 65552 | tf_op jit(solution)/shard_map/reduce_scatter | solution.py:177
  1029.0 156.1 %reduce-scatter.13.cloned.1.call-done = bf16[32,512]{1,0:T(8,128)(2,1)} async-done(((bf16[1024,512]{1,0:T(8,128)(2,1)}), bf16[32,512]{1,0:T(8,128)(2,1)}) %reduce-scatter.13.cloned.1.call-update) | async-done | bytes 32784 | tf_op jit(solution)/shard_map/reduce_scatter | solution.py:171
  1186.5 158.7 %reduce-scatter.15.cloned.1.call-done = bf16[32,512]{1,0:T(8,128)(2,1)} async-done(((bf16[1024,512]{1,0:T(8,128)(2,1)}), bf16[32,512]{1,0:T(8,128)(2,1)}) %reduce-scatter.15.cloned.1.call-update) | async-done | bytes 32784 | tf_op jit(solution)/shard_map/reduce_scatter | solution.py:174
  (178 shorter events, 130.3 us)
Async XLA Ops:
  7.2 266.7 %copy-start = (bf16[1,512,2048]{2,1,0:T(8,128)(2,1)S(1)}, bf16[1,512,2048]{2,1,0:T(8,128)(2,1)}, u32[]{:S(2)}) copy-start(bf16[1,512,2048]{2,1,0:T(8,128)(2,1)} %param.17) | copy-start | bytes 6291460
  7.2 3.7 copy-start.2
  7.2 216.8 %all-gather.2.cloned.1.call-start = ((), (), s32[]{:S(2)}) async-start(), calls=%async_computation.7 | async-start | bytes 4595712 | tf_op jit(solution)/shard_map/all_gather | solution.py:85
  8.5 7.4 copy-start.9
  18.7 9.6 copy-start.7
  18.7 75.4 %all-to-all-start = ((bf16[32,136,512]{2,1,0:T(8,128)(2,1)}), bf16[32,136,512]{2,1,0:T(8,128)(2,1)}, u32[]{:S(2)}, u32[]{:S(2)}) async-start(bf16[32,136,512]{2,1,0:T(8,128)(2,1)} %stack.2), calls=%async_computation | async-start | bytes 8912896 | tf_op jit(solution)/shard_map/all_to_all | solution.py:13
  28.2 505.2 %reduce-scatter.19.cloned.1.call-start = ((), (), s32[]{:S(2)}) async-start(), calls=%async_computation.12 | async-start | bytes 4595712
  28.3 4.2 copy-start.24
  230.4 9.2 copy-start.22
  363.8 338.4 %reduce-scatter.21.cloned.1.call-start = ((), (), s32[]{:S(2)}) async-start(), calls=%async_computation.13 | async-start | bytes 4595712
  370.3 1.0 copy-start.6
  370.3 1.2 copy-start.13
  370.4 493.5 %reduce-scatter.11.cloned.1.call-start = ((), (), s32[]{:S(2)}) async-start(), calls=%async_computation.8 | async-start | bytes 1081344 | tf_op jit(solution)/shard_map/reduce_scatter | solution.py:168
  371.5 1.9 copy-start.14
  371.5 1.9 copy-start.17
  371.5 1.9 copy-start.19
  373.3 161.1 %copy-start.4 = (f32[136,8,64]{0,2,1:T(8,128)S(1)}, f32[136,8,64]{0,2,1:T(8,128)}, u32[]{:S(2)}) copy-start(f32[136,8,64]{0,2,1:T(8,128)} %copy-done.3) | copy-start | bytes 835588
  373.3 652.5 %reduce-scatter.17.cloned.1.call-start = ((), (), s32[]{:S(2)}) async-start(), calls=%async_computation.11 | async-start | bytes 2162688 | tf_op jit(solution)/shard_map/reduce_scatter | solution.py:177
  375.5 161.5 %copy-start.8 = (bf16[1,1024,512]{2,1,0:T(8,128)(2,1)S(1)}, bf16[1,1024,512]{2,1,0:T(8,128)(2,1)}, u32[]{:S(2)}) copy-start(bf16[1,1024,512]{2,1,0:T(8,128)(2,1)} %param.14) | copy-start | bytes 3145732
  375.5 809.6 %reduce-scatter.13.cloned.1.call-start = ((), (), s32[]{:S(2)}) async-start(), calls=%async_computation.9 | async-start | bytes 1081344 | tf_op jit(solution)/shard_map/reduce_scatter | solution.py:171
  536.9 0.9 copy-start.12
  536.9 808.3 %reduce-scatter.15.cloned.1.call-start = ((), (), s32[]{:S(2)}) async-start(), calls=%async_computation.10 | async-start | bytes 1081344 | tf_op jit(solution)/shard_map/reduce_scatter | solution.py:174
  537.8 166.2 %copy-start.15 = (bf16[1,136,1024]{2,1,0:T(8,128)(2,1)S(1)}, bf16[1,136,1024]{2,1,0:T(8,128)(2,1)}, u32[]{:S(2)}) copy-start(bf16[1,136,1024]{2,1,0:T(8,128)(2,1)} %param.13) | copy-start | bytes 835588
  702.1 5.7 copy-start.21
  704.0 18.6 %copy-start.23 = (s32[1,136]{1,0:T(1,128)S(1)}, s32[1,136]{1,0:T(1,128)}, u32[]{:S(2)}) copy-start(s32[1,136]{1,0:T(1,128)} %param.19) | copy-start | bytes 1636
  704.3 3.5 collective-permute-start
  707.8 6.7 collective-permute-start.1
  707.8 638.8 %copy-start.1 = (bf16[1,512,2048]{2,1,0:T(8,128)(2,1)S(1)}, bf16[1,512,2048]{2,1,0:T(8,128)(2,1)}, u32[]{:S(2)}) copy-start(bf16[1,512,2048]{2,1,0:T(8,128)(2,1)} %param.17) | copy-start | bytes 6291460
  714.5 8.1 collective-permute-start.2
  722.7 7.0 collective-permute-start.3
  729.6 135.6 %collective-permute-start.4 = (bf16[136,1024]{1,0:T(8,128)(2,1)S(1)}, bf16[136,1024]{1,0:T(8,128)(2,1)S(1)}, u32[]{:S(2)}, u32[]{:S(2)}) collective-permute-start(bf16[136,1024]{1,0:T(8,128)(2,1)S(1)} %collective-permute-done.3), channel_id=1, source_target_pairs={{0,8},{8,0},{1,9},{9,1},{2,10},{10,2},{3,11},{11,3},{4,12},{12,4},... | collective-permute-start | bytes 835592 | tf_op jit(solution)/shard_map/ppermute | solution.py:23
  865.3 162.1 %collective-permute-start.5 = (bf16[136,1024]{1,0:T(8,128)(2,1)S(1)}, bf16[136,1024]{1,0:T(8,128)(2,1)S(1)}, u32[]{:S(2)}, u32[]{:S(2)}) collective-permute-start(bf16[136,1024]{1,0:T(8,128)(2,1)S(1)} %collective-permute-done.4), channel_id=1, source_target_pairs={{0,16},{16,0},{1,17},{17,1},{2,18},{18,2},{3,19},{19,3},{4,20},{20... | collective-permute-start | bytes 835592 | tf_op jit(solution)/shard_map/ppermute | solution.py:23
  (7 other events, 5.3 us)
Sparse Core Ops, SparseCore 0:
  16.1 207.8 all-gather.1
  363.9 169.4 reduce-scatter.18
  535.9 166.1 reduce-scatter.20
  704.3 159.5 reduce-scatter.10
  866.2 159.5 reduce-scatter.16
  1028.1 157.0 reduce-scatter.12
  1187.6 157.5 reduce-scatter.14
